TPU v7x, 512 devices: a whole 4x8x8 slice. The times are simulated.
512 devices in a mesh: ctx: 32 (over x, y), head: 16 (over z, core).
Axes of the slice: x: 4, y: 8, z: 8, core: 2. Of those that a mesh axis runs over, the one named last changes fastest.
Arguments:
- queries: bfloat16 [8192, 4096], P('ctx', 'head'), may hold values from -6 to 6
- keys_values: bfloat16 [8192, 1024], P('ctx'), may hold values from -6 to 6
- grad_rows: bfloat16 [8192, 2880], P('ctx', 'head'), may hold values from -6 to 6
- doc_ids: int32 [8192], replicated, may hold values from 0 to 7, never falling along the last dimension, each value on 1 to 2048 neighbouring positions
- tile_list: int32 [64], replicated, may hold values from 0 to 63, each once
Outputs:
- attended: float32 [8192, 4096], P('ctx', 'head')
- weight_grad: float32 [2880, 4096], P('ctx', 'head')
Inputs may be any that keep to these rules, and one draw needn't show every extreme that they name: `tile_list`: every slot index names a different tile. `doc_ids`: never falling along the window; each document holds 1 to 2048 positions.
All inputs are finite; a program needn't handle non-finite values.
Results may differ from a plain program's by a relative error of at most 0.0018.
Values may be sent and summed in bfloat16 or wider, within the bound.
No kernel may reach another device: no remote copies, remote signals or barrier semaphores. Data moves between devices by JAX's collectives and lax.ppermute only.
A program may use at most 128 MiB of HBM per device.

v0:
```python
import jax
import jax.numpy as jnp
from jax import lax
from jax.sharding import PartitionSpec as P

H = 64
KVH = 8
DH = 64
TILE = 128
NEG_FILL = -1e30


def on_device(queries, keys_values, grad_rows, doc_ids, tile_list):
    tokens_local = queries.shape[0]
    heads_local = queries.shape[1] // DH
    group = H // KVH
    kv_local = max(1, heads_local // group)
    per_kv = heads_local // kv_local
    scale = DH ** (-0.5)
    head_index = lax.axis_index("head")
    kv_start = head_index * heads_local // group
    own_kv = lax.dynamic_slice_in_dim(keys_values, kv_start * 2 * DH, kv_local * 2 * DH, 1)
    tile_count = tile_list.shape[0]
    offsets = jnp.arange(TILE, dtype=jnp.int32)
    slot_pos = (tile_list[:, None] * TILE + offsets[None, :]).reshape(-1)
    slot_doc = doc_ids.reshape(tile_count, TILE)[tile_list].reshape(-1)
    row_start = lax.axis_index("ctx") * tokens_local
    query_pos = lax.dynamic_slice_in_dim(slot_pos, row_start, tokens_local)
    query_doc = lax.dynamic_slice_in_dim(slot_doc, row_start, tokens_local)
    grouped = queries.reshape(tokens_local, kv_local, per_kv, DH)
    piece = lax.all_gather(own_kv, "ctx", axis=0, tiled=True)
    count = piece.shape[0]
    allowed = (query_doc[:, None] == slot_doc[None, :]) & (slot_pos[None, :] <= query_pos[:, None])
    run_max = jnp.full((kv_local, per_kv, tokens_local), NEG_FILL, jnp.float32)
    parts = piece.reshape(count, kv_local, 2, DH)
    keys = parts[:, :, 0]
    values = parts[:, :, 1]
    scores = jnp.einsum("tgqd,ngd->gqtn", grouped, keys, preferred_element_type=jnp.float32) * scale
    masked = jnp.where(allowed, scores, NEG_FILL)
    new_max = jnp.maximum(run_max, jnp.max(masked, axis=-1))
    weights = jnp.where(allowed, jnp.exp(masked - new_max[..., None]), 0.0)
    new_sum = jnp.sum(weights, axis=-1)
    added = jnp.einsum(
        "gqtn,ngd->gqtd", weights.astype(jnp.bfloat16), values, preferred_element_type=jnp.float32
    )
    normed = added / new_sum[..., None]
    attended = jnp.transpose(normed, (2, 0, 1, 3)).reshape(tokens_local, heads_local * DH)
    term = lax.dot_general(
        lax.all_gather(grad_rows, "head", axis=1, tiled=True).astype(jnp.float32),
        attended,
        (((0,), (0,)), ((), ())),
        precision=lax.Precision.HIGHEST,
        preferred_element_type=jnp.float32,
    )
    summed = lax.psum(term, "ctx")
    share = summed.shape[0] // lax.axis_size("ctx")
    weight_grad = lax.dynamic_slice_in_dim(summed, lax.axis_index("ctx") * share, share, 0)
    return (attended, weight_grad)


def solution(mesh):
    in_specs = (P("ctx", "head"), P("ctx", None), P("ctx", "head"), P(), P())
    out_specs = (P("ctx", "head"), P("ctx", "head"))
    return jax.shard_map(
        on_device, mesh=mesh, in_specs=in_specs, out_specs=out_specs, check_vma=False
    )
```

profile of v0, /device:TPU:16, one launch (start us, length us, event | category | flops | bytes accessed | tf_op | source)
XLA Modules:
  0.0 366.6 jit_solution(1659560030699857460)
XLA Ops:
  7.2 0.0 all-gather.6.cloned.1.call-start
  7.2 0.7 all-gather.6.cloned.1.call-update
  7.9 0.0 all-gather.4.cloned.1.call-start
  8.0 0.2 copy-done
  8.2 0.6 constant_dynamic-slice_fusion.1
  8.9 0.0 all-reduce.2.cloned.1.call-start
  8.9 0.7 compare_select_fusion
  9.6 1.4 gather_fusion
  11.0 0.1 dynamic_slice.12
  11.0 0.1 add_bitcast_fusion
  11.1 0.1 dynamic_slice.13
  11.2 1.0 copy.16
  12.2 5.7 %compare_and_fusion = pred[256,8192]{0,1:T(8,128)(4,1)S(1)} fusion(s32[256]{0:T(256)S(1)} %dynamic_slice.13, s32[256]{0:T(256)S(1)} %dynamic_slice.12, s32[8192]{0:T(1024)S(1)} %add_bitcast_fusion, s32[8192]{0:T(1024)S(1)} %bitcast.59), kind=kLoop, calls=%fused_computation.9 | loop fusion | flops 6291456 | bytes 2164736 | tf_op jit(solution)/shard_map/and | solution.py:33
  17.9 39.0 %all-gather.6.cloned.1.call-done = bf16[16,180,256]{2,1,0:T(8,128)(2,1)} async-done(((bf16[1,180,256]{2,1,0:T(8,128)(2,1)}), bf16[16,180,256]{2,1,0:T(8,128)(2,1)}) %all-gather.6.cloned.1.call-update) | async-done | bytes 1474576 | tf_op jit(solution)/shard_map/all_gather | solution.py:49
  56.9 3.3 reshape.91
  60.2 81.3 %all-gather.4.cloned.1.call-done = bf16[8192,128]{1,0:T(8,128)(2,1)} async-done(((bf16[256,128]{1,0:T(8,128)(2,1)}), bf16[8192,128]{1,0:T(8,128)(2,1)}) %all-gather.4.cloned.1.call-update) | async-done | bytes 2097168 | tf_op jit(solution)/shard_map/all_gather | solution.py:31
  141.4 4.1 %copy.15 = bf16[8192,128]{0,1:T(8,128)(2,1)} copy(bf16[8192,128]{1,0:T(8,128)(2,1)} %all-gather.4.cloned.1.call-done) | data formatting | bytes 4194304 | tf_op jit(solution)/shard_map/all_gather | solution.py:31
  145.5 14.5 %fusion = (f32[4,256]{1,0:T(4,128)S(1)}, f32[8192,256,4]{1,0,2:T(8,128)}) fusion(pred[256,8192]{0,1:T(8,128)(4,1)S(1)} %compare_and_fusion, bf16[256,4,64]{0,2,1:T(8,128)(2,1)S(1)} %bitcast.60, bf16[8192,1,2,64]{0,3,2,1:T(8,128)(2,1)} %bitcast.54), kind=kOutput, calls=%fused_computation.3 | convolution fusion | flops 1098906624 | bytes 36835328 | tf_op jit(solution)/shard_map/tgqd,ngd->gqtn/dot_general | solution.py:38
  160.0 15.0 %fusion.1 = f32[4,256]{1,0:T(4,128)S(1)} fusion(f32[8192,256,4]{1,0,2:T(8,128)} %get-tuple-element.11, f32[4,256]{1,0:T(4,128)S(1)} %broadcast_maximum_fusion, pred[256,8192]{0,1:T(8,128)(4,1)S(1)} %compare_and_fusion), kind=kLoop, calls=%fused_computation.4 | loop fusion | flops 41942016 | bytes 35659776 | tf_op jit(solution)/shard_map/reduce_sum | solution.py:42
  175.0 14.5 %fusion.7 = f32[4,256,64]{1,2,0:T(8,128)S(1)} fusion(f32[8192,256,4]{1,0,2:T(8,128)} %get-tuple-element.11, f32[4,256]{1,0:T(4,128)S(1)} %broadcast_maximum_fusion, pred[256,8192]{0,1:T(8,128)(4,1)S(1)} %compare_and_fusion, bf16[8192,1,2,64]{0,3,2,1:T(8,128)(2,1)} %bitcast.55, f32[4,256]{1,0:T(4,128)S(1)} %fusion.1), kind=kOutput, calls=%fused_computation.11 | convolution fusion | flops 1115750400 | bytes 36970496 | tf_op jit(solution)/shard_map/gqtn,ngd->gqtd/dot_general | solution.py:43
  189.5 3.0 convolution_bitcast_fusion
  192.6 0.8 copy.18
  193.4 165.1 %all-reduce.2.cloned.1.call-done = f32[2880,256]{1,0:T(8,128)} async-done(((f32[2880,256]{1,0:T(8,128)}), f32[2880,256]{1,0:T(8,128)}) %all-reduce.2.cloned.1.call-update) | async-done | bytes 2949136 | tf_op jit(solution)/shard_map/psum | solution.py:55
  358.5 1.5 constant_dynamic-slice_fusion
  (7 shorter events, 0.1 us)
Async XLA Ops:
  7.2 1.0 copy-start
  7.2 49.7 %all-gather.6.cloned.1.call-start = ((), (), s32[]{:S(2)}) async-start(), calls=%async_computation.2 | async-start | bytes 1601536 | tf_op jit(solution)/shard_map/all_gather | solution.py:49
  7.9 133.5 %all-gather.4.cloned.1.call-start = ((), (), s32[]{:S(2)}) async-start(), calls=%async_computation | async-start | bytes 2162688 | tf_op jit(solution)/shard_map/all_gather | solution.py:31
  8.9 349.6 %all-reduce.2.cloned.1.call-start = ((), (), s32[]{:S(2)}) async-start(), calls=%async_computation.1 | async-start | bytes 5898240 | tf_op jit(solution)/shard_map/psum | solution.py:55
  175.0 14.5 %copy-start.1 = (bf16[2880,256]{1,0:T(8,128)(2,1)S(1)}, bf16[2880,256]{1,0:T(8,128)(2,1)}, u32[]{:S(2)}) copy-start(bf16[2880,256]{1,0:T(8,128)(2,1)} %reshape.91) | copy-start | bytes 4423684
Sparse Core Ops, SparseCore 0:
  10.1 46.7 all-gather.5
  60.6 80.7 all-gather.3
  192.7 165.7 all-reduce.1
where the time goes:
time: 367 us
  waiting for transfers between devices  286 us (78%)
  matrix products  32 us (9%)
  other arithmetic  21.4 us (6%)
  between operations  13.8 us (4%)
  local copies, waits for them, and re-layouts  13.2 us (4%)
    psum x1, waiting for transfers between devices, on_device(): summed = lax.psum(term, 'ctx')  165 us
    all_gather x1, waiting for transfers between devices, on_device(): piece = lax.all_gather(own_kv, 'ctx', axis=0, tiled=True)  81.3 us
    all_gather x1, waiting for transfers between devices, on_device(): lax.all_gather(grad_rows, 'head', axis=1, tiled=True).astype(jnp.float32)  39 us
    reduce_sum x1, other arithmetic, on_device(): new_sum = jnp.sum(weights, axis=-1)  15 us
    dot_general x1, matrix products, on_device(): jnp.einsum('gqtn,ngd->gqtd', weights.astype(jnp.bfloat16), values, prefer...  14.5 us
    dot_general x1, matrix products, on_device(): jnp.einsum('tgqd,ngd->gqtn', grouped, keys, preferred_element_type=jnp.fl...  14.5 us
  transfers between devices with their start and end apart: 3, of which 3 were waited for; matrix products, arithmetic and copies ran while one was open for 4% of the time, Pallas kernels for 0%

commit v1 on v0

--- a/solution.py
+++ b/solution.py
@@ -52,7 +52,9 @@
         precision=lax.Precision.HIGHEST,
         preferred_element_type=jnp.float32,
     )
-    summed = lax.psum(term, "ctx")
+    summed = term
+    for hop in (1, 2, 4, 8, 16):
+        summed = summed + lax.ppermute(summed, "ctx", [(dev, dev ^ hop) for dev in range(32)])
     share = summed.shape[0] // lax.axis_size("ctx")
     weight_grad = lax.dynamic_slice_in_dim(summed, lax.axis_index("ctx") * share, share, 0)
     return (attended, weight_grad)

time: 367 us -> 660 us (1.80)
  the two profiles are of different devices: /device:TPU:16 before, /device:TPU:24 now
where the time goes in v1:
time: 660 us
  waiting for transfers between devices  563 us (85%)
  matrix products  30.3 us (5%)
  other arithmetic  24.5 us (4%)
  starting transfers between devices  14.7 us (2%)
  between operations  14.2 us (2%)
  local copies, waits for them, and re-layouts  12.6 us (2%)
    ppermute x5, waiting for transfers between devices, on_device(): lax.ppermute(summed, 'ctx', [(dev, dev ^ hop) for dev in range(32)])  443 us
    all_gather x1, waiting for transfers between devices, on_device(): piece = lax.all_gather(own_kv, 'ctx', axis=0, tiled=True)  80.5 us
    all_gather x1, waiting for transfers between devices, on_device(): lax.all_gather(grad_rows, 'head', axis=1, tiled=True).astype(jnp.float32)  39 us
    reduce_sum x1, other arithmetic, on_device(): new_sum = jnp.sum(weights, axis=-1)  15 us
    ppermute x5, starting transfers between devices, on_device(): lax.ppermute(summed, 'ctx', [(dev, dev ^ hop) for dev in range(32)])  14.6 us
    dot_general x1, matrix products, on_device(): jnp.einsum('gqtn,ngd->gqtd', weights.astype(jnp.bfloat16), values, prefer...  14.5 us
    dot_general x1, matrix products, on_device(): jnp.einsum('tgqd,ngd->gqtn', grouped, keys, preferred_element_type=jnp.fl...  14.5 us
  transfers between devices with their start and end apart: 7, of which 7 were waited for; matrix products, arithmetic and copies ran while one was open for 2% of the time, Pallas kernels for 0%

profile of v1, /device:TPU:24, one launch (start us, length us, event | category | flops | bytes accessed | tf_op | source)
XLA Modules:
  0.0 659.6 jit_solution(18230904816165321410)
XLA Ops:
  7.2 0.7 all-gather.6.cloned.1.call-update
  9.6 1.4 gather_fusion
  11.1 1.0 copy.16
  12.2 5.7 compare_and_fusion
  17.8 39.0 %all-gather.6.cloned.1.call-done = bf16[16,180,256]{2,1,0:T(8,128)(2,1)} async-done(((bf16[1,180,256]{2,1,0:T(8,128)(2,1)}), bf16[16,180,256]{2,1,0:T(8,128)(2,1)}) %all-gather.6.cloned.1.call-update) | async-done | bytes 1474576 | tf_op jit(solution)/shard_map/all_gather | solution.py:49
  56.8 3.3 reshape.91
  60.1 80.5 %all-gather.4.cloned.1.call-done = bf16[8192,128]{1,0:T(8,128)(2,1)} async-done(((bf16[256,128]{1,0:T(8,128)(2,1)}), bf16[8192,128]{1,0:T(8,128)(2,1)}) %all-gather.4.cloned.1.call-update) | async-done | bytes 2097168 | tf_op jit(solution)/shard_map/all_gather | solution.py:31
  140.6 4.1 copy.15
  144.7 14.5 %fusion = (f32[4,256]{1,0:T(4,128)S(1)}, f32[8192,256,4]{1,0,2:T(8,128)}) fusion(pred[256,8192]{0,1:T(8,128)(4,1)S(1)} %compare_and_fusion, bf16[256,4,64]{0,2,1:T(8,128)(2,1)S(1)} %bitcast.60, bf16[8192,1,2,64]{0,3,2,1:T(8,128)(2,1)} %bitcast.54), kind=kOutput, calls=%fused_computation.3 | convolution fusion | flops 1098906624 | bytes 36835328 | tf_op jit(solution)/shard_map/tgqd,ngd->gqtn/dot_general | solution.py:38
  159.1 15.0 %fusion.1 = f32[4,256]{1,0:T(4,128)S(1)} fusion(f32[8192,256,4]{1,0,2:T(8,128)} %get-tuple-element.11, f32[4,256]{1,0:T(4,128)S(1)} %broadcast_maximum_fusion, pred[256,8192]{0,1:T(8,128)(4,1)S(1)} %compare_and_fusion), kind=kLoop, calls=%fused_computation.4 | loop fusion | flops 41942016 | bytes 35659776 | tf_op jit(solution)/shard_map/reduce_sum | solution.py:42
  174.1 14.5 %fusion.7 = f32[4,256,64]{1,2,0:T(8,128)S(1)} fusion(f32[8192,256,4]{1,0,2:T(8,128)} %get-tuple-element.11, f32[4,256]{1,0:T(4,128)S(1)} %broadcast_maximum_fusion, pred[256,8192]{0,1:T(8,128)(4,1)S(1)} %compare_and_fusion, bf16[8192,1,2,64]{0,3,2,1:T(8,128)(2,1)} %bitcast.55, f32[4,256]{1,0:T(4,128)S(1)} %fusion.1), kind=kOutput, calls=%fused_computation.11 | convolution fusion | flops 1115750400 | bytes 36970496 | tf_op jit(solution)/shard_map/gqtn,ngd->gqtd/dot_general | solution.py:43
  188.6 1.4 convolution_bitcast_fusion
  190.0 3.2 collective-permute-start
  193.2 60.1 %collective-permute-done = f32[2880,256]{1,0:T(8,128)S(1)} collective-permute-done((f32[2880,256]{1,0:T(8,128)S(1)}, f32[2880,256]{1,0:T(8,128)S(1)}, u32[]{:S(2)}, u32[]{:S(2)}) %collective-permute-start) | collective-permute-done | bytes 2949152 | tf_op jit(solution)/shard_map/ppermute | solution.py:57
  253.7 2.8 collective-permute-start.1
  256.5 123.7 %collective-permute-done.1 = f32[2880,256]{1,0:T(8,128)S(1)} collective-permute-done((f32[2880,256]{1,0:T(8,128)S(1)}, f32[2880,256]{1,0:T(8,128)S(1)}, u32[]{:S(2)}, u32[]{:S(2)}) %collective-permute-start.1) | collective-permute-done | bytes 2949152 | tf_op jit(solution)/shard_map/ppermute | solution.py:57
  380.6 4.7 collective-permute-start.2
  385.3 129.3 %collective-permute-done.2 = f32[2880,256]{1,0:T(8,128)S(1)} collective-permute-done((f32[2880,256]{1,0:T(8,128)S(1)}, f32[2880,256]{1,0:T(8,128)S(1)}, u32[]{:S(2)}, u32[]{:S(2)}) %collective-permute-start.2) | collective-permute-done | bytes 2949152 | tf_op jit(solution)/shard_map/ppermute | solution.py:57
  515.0 1.9 collective-permute-start.3
  517.0 65.6 %collective-permute-done.3 = f32[2880,256]{1,0:T(8,128)S(1)} collective-permute-done((f32[2880,256]{1,0:T(8,128)S(1)}, f32[2880,256]{1,0:T(8,128)S(1)}, u32[]{:S(2)}, u32[]{:S(2)}) %collective-permute-start.3) | collective-permute-done | bytes 2949152 | tf_op jit(solution)/shard_map/ppermute | solution.py:57
  583.0 1.9 collective-permute-start.4
  584.9 1.8 copy.18
  586.7 64.6 %collective-permute-done.4 = f32[2880,256]{1,0:T(8,128)} collective-permute-done((f32[2880,256]{1,0:T(8,128)S(1)}, f32[2880,256]{1,0:T(8,128)}, u32[]{:S(2)}, u32[]{:S(2)}) %collective-permute-start.4) | collective-permute-done | bytes 2949152 | tf_op jit(solution)/shard_map/ppermute | solution.py:57
  651.2 1.6 dynamic-slice_add_fusion
  (22 shorter events, 3.4 us)
Async XLA Ops:
  7.2 1.1 copy-start
  7.2 49.6 %all-gather.6.cloned.1.call-start = ((), (), s32[]{:S(2)}) async-start(), calls=%async_computation.1 | async-start | bytes 1601536 | tf_op jit(solution)/shard_map/all_gather | solution.py:49
  7.9 132.7 %all-gather.4.cloned.1.call-start = ((), (), s32[]{:S(2)}) async-start(), calls=%async_computation | async-start | bytes 2162688 | tf_op jit(solution)/shard_map/all_gather | solution.py:31
  174.1 14.5 %copy-start.2 = (bf16[2880,256]{1,0:T(8,128)(2,1)S(1)}, bf16[2880,256]{1,0:T(8,128)(2,1)}, u32[]{:S(2)}) copy-start(bf16[2880,256]{1,0:T(8,128)(2,1)} %reshape.91) | copy-start | bytes 4423684
  188.6 67.9 %copy-start.3 = (f32[4,256,64]{1,2,0:T(8,128)}, f32[4,256,64]{1,2,0:T(8,128)S(1)}, u32[]{:S(2)}) copy-start(f32[4,256,64]{1,2,0:T(8,128)S(1)} %fusion.7) | copy-start | bytes 786436
  190.0 63.3 %collective-permute-start = (f32[2880,256]{1,0:T(8,128)S(1)}, f32[2880,256]{1,0:T(8,128)S(1)}, u32[]{:S(2)}, u32[]{:S(2)}) collective-permute-start(f32[2880,256]{1,0:T(8,128)S(1)} %convolution_bitcast_fusion), channel_id=1, source_target_pairs={{0,16},{16,0},{32,48},{48,32},{64,80},{80,64},{96,112},{112,96},{1... | collective-permute-start | bytes 8847368 | tf_op jit(solution)/shard_map/ppermute | solution.py:57
  253.7 126.5 %collective-permute-start.1 = (f32[2880,256]{1,0:T(8,128)S(1)}, f32[2880,256]{1,0:T(8,128)S(1)}, u32[]{:S(2)}, u32[]{:S(2)}) collective-permute-start(f32[2880,256]{1,0:T(8,128)S(1)} %add.61), channel_id=1, source_target_pairs={{0,32},{16,48},{32,0},{48,16},{64,96},{80,112},{96,64},{112,80},{1... | collective-permute-start | bytes 8847368 | tf_op jit(solution)/shard_map/ppermute | solution.py:57
  380.2 272.6 %copy-start.1 = (bf16[256,1024]{1,0:T(8,128)(2,1)S(1)}, bf16[256,1024]{1,0:T(8,128)(2,1)}, u32[]{:S(2)}) copy-start(bf16[256,1024]{1,0:T(8,128)(2,1)} %param.6) | copy-start | bytes 1572868
  380.6 134.1 %collective-permute-start.2 = (f32[2880,256]{1,0:T(8,128)S(1)}, f32[2880,256]{1,0:T(8,128)S(1)}, u32[]{:S(2)}, u32[]{:S(2)}) collective-permute-start(f32[2880,256]{1,0:T(8,128)S(1)} %add.62), channel_id=1, source_target_pairs={{0,64},{16,80},{32,96},{48,112},{64,0},{80,16},{96,32},{112,48},{1... | collective-permute-start | bytes 8847368 | tf_op jit(solution)/shard_map/ppermute | solution.py:57
  515.0 67.5 %collective-permute-start.3 = (f32[2880,256]{1,0:T(8,128)S(1)}, f32[2880,256]{1,0:T(8,128)S(1)}, u32[]{:S(2)}, u32[]{:S(2)}) collective-permute-start(f32[2880,256]{1,0:T(8,128)S(1)} %add.63), channel_id=1, source_target_pairs={{0,128},{16,144},{32,160},{48,176},{64,192},{80,208},{96,224},{112... | collective-permute-start | bytes 8847368 | tf_op jit(solution)/shard_map/ppermute | solution.py:57
  583.0 68.3 %collective-permute-start.4 = (f32[2880,256]{1,0:T(8,128)S(1)}, f32[2880,256]{1,0:T(8,128)}, u32[]{:S(2)}, u32[]{:S(2)}) collective-permute-start(f32[2880,256]{1,0:T(8,128)S(1)} %add.64), channel_id=1, source_target_pairs={{0,256},{16,272},{32,288},{48,304},{64,320},{80,336},{96,352},{112... | collective-permute-start | bytes 8847368 | tf_op jit(solution)/shard_map/ppermute | solution.py:57
Sparse Core Ops, SparseCore 0:
  10.1 46.6 all-gather.5
  60.5 80.0 all-gather.3
